TPU v7x, 32 devices: a whole 2x2x4 slice. The times are simulated.
32 devices in a mesh: dp: 16 (over z, y, core), tensor: 2 (over x).
Axes of the slice: x: 2, y: 2, z: 4, core: 2. Of those that a mesh axis runs over, the one named last changes fastest.
Arguments:
- patches: bfloat16 [50176, 768], P(('dp', 'tensor')), may hold values from -6 to 6
- visible: int32 [1024, 49], P(('dp', 'tensor')), may hold values from 0 to 195, as said below
- pos_table: float32 [196, 768], replicated, may hold values from -6 to 6
- cotangent: bfloat16 [50176, 768], P(('dp', 'tensor')), may hold values from -6 to 6
- step_count: int32 [1], replicated, may hold values from 2 to 20
- w_qkv: float32 [768, 3, 768], P('dp', None, 'tensor'), may hold values from -0.21875 to 0.21875
- m_qkv: float32 [768, 3, 768], P('dp', None, 'tensor'), may hold values from -0.00018793954 to 0.00018793954
- v_qkv: float32 [768, 3, 768], P('dp', None, 'tensor'), may hold values from 7.48811e-09 to 2.9669868e-08
- w_proj: float32 [768, 768], P('tensor', 'dp'), may hold values from -0.875 to 0.875
- m_proj: float32 [768, 768], P('tensor', 'dp'), may hold values from -0.00018793954 to 0.00018793954
- v_proj: float32 [768, 768], P('tensor', 'dp'), may hold values from 7.48811e-09 to 2.9669868e-08
- w_fc1: float32 [768, 4, 768], P('dp', None, 'tensor'), may hold values from -0.21875 to 0.21875
- m_fc1: float32 [768, 4, 768], P('dp', None, 'tensor'), may hold values from -0.00018793954 to 0.00018793954
- v_fc1: float32 [768, 4, 768], P('dp', None, 'tensor'), may hold values from 7.48811e-09 to 2.9669868e-08
- w_fc2: float32 [4, 768, 768], P(None, 'tensor', 'dp'), may hold values from -0.109375 to 0.109375
- m_fc2: float32 [4, 768, 768], P(None, 'tensor', 'dp'), may hold values from -0.00018793954 to 0.00018793954
- v_fc2: float32 [4, 768, 768], P(None, 'tensor', 'dp'), may hold values from 7.48811e-09 to 2.9669868e-08
- split_bias: float32 [6, 768], P(None, 'tensor'), may hold values from -3 to 3
- m_split: float32 [6, 768], P(None, 'tensor'), may hold values from -0.0005638186 to 0.0005638186
- v_split: float32 [6, 768], P(None, 'tensor'), may hold values from 6.640399e-08 to 2.6844165e-07
- norm_bias: float32 [6, 768], replicated, may hold values from -1.2 to 1.8
- m_norm: float32 [6, 768], replicated, may hold values from -0.0005638186 to 0.0005638186
- v_norm: float32 [6, 768], replicated, may hold values from 6.640399e-08 to 2.6844165e-07
Outputs:
- block_out: bfloat16 [50176, 768], P(('dp', 'tensor'))
- input_grad: float32 [50176, 768], P(('dp', 'tensor'))
- grad_norm: float32 [], replicated
- new_qkv: float32 [768, 3, 768], P('dp', None, 'tensor')
- first_qkv: float32 [768, 3, 768], P('dp', None, 'tensor')
- second_qkv: float32 [768, 3, 768], P('dp', None, 'tensor')
- new_proj: float32 [768, 768], P('tensor', 'dp')
- first_proj: float32 [768, 768], P('tensor', 'dp')
- second_proj: float32 [768, 768], P('tensor', 'dp')
- new_fc1: float32 [768, 4, 768], P('dp', None, 'tensor')
- first_fc1: float32 [768, 4, 768], P('dp', None, 'tensor')
- second_fc1: float32 [768, 4, 768], P('dp', None, 'tensor')
- new_fc2: float32 [4, 768, 768], P(None, 'tensor', 'dp')
- first_fc2: float32 [4, 768, 768], P(None, 'tensor', 'dp')
- second_fc2: float32 [4, 768, 768], P(None, 'tensor', 'dp')
- new_split: float32 [6, 768], P(None, 'tensor')
- first_split: float32 [6, 768], P(None, 'tensor')
- second_split: float32 [6, 768], P(None, 'tensor')
- new_norm: float32 [6, 768], replicated
- first_norm: float32 [6, 768], replicated
- second_norm: float32 [6, 768], replicated
Inputs may be any that keep to these rules, and one draw needn't show every extreme that they name: `visible`: the 49 entries of an image are distinct patch positions.
All inputs are finite; a program needn't handle non-finite values.
Results may differ from a plain program's by a relative error of at most 0.014.
Values may be sent and summed in bfloat16 or wider, within the bound.
No kernel may reach another device: no remote copies, remote signals or barrier semaphores. Data moves between devices by JAX's collectives and lax.ppermute only.
A program may use at most 256 MiB of HBM per device.

v0:
```python
from functools import partial

import jax
import jax.numpy as jnp
from jax import lax
from jax.sharding import PartitionSpec as P

HD = 64
VISIBLE = 49


norm_eps = 1e-06
beta_one = 0.9
beta_two = 0.95
adam_eps = 1e-08
clip_value = 1.0
matrix_rate = 0.02
proj_rate = 0.08
vector_rate = 0.2
matrix_decay = 0.05


def layer_norm(values, row_gain, row_shift):
    row_mean = jnp.mean(values, axis=-1, keepdims=True)
    centred = values - row_mean
    variance = jnp.mean(centred * centred, axis=-1, keepdims=True)
    return centred * lax.rsqrt(variance + norm_eps) * row_gain + row_shift


def adam_update(
    weight, gradient, first_moment, second, factor, bias_first, bias_second, learn_rate, decay_rate
):
    clipped = gradient * factor
    first_new = beta_one * first_moment + (1.0 - beta_one) * clipped
    second_new = beta_two * second + (1.0 - beta_two) * clipped * clipped
    direction = first_new / bias_first / (jnp.sqrt(second_new / bias_second) + adam_eps)
    return (weight - learn_rate * (direction + decay_rate * weight), first_new, second_new)


def transpose_dot(left_side, right_side):
    return lax.dot_general(
        left_side, right_side, (((0,), (0,)), ((), ())), preferred_element_type=jnp.float32
    )


def dot_back(left_side, right_side):
    return lax.dot_general(
        left_side, right_side, (((1,), (1,)), ((), ())), preferred_element_type=jnp.float32
    )


def square_sum(arrays):
    total = jnp.sum(arrays[0] * arrays[0])
    for member in arrays[1:]:
        total = total + jnp.sum(member * member)
    return total


def body(
    patches,
    visible,
    pos_table,
    cotangent,
    step_count,
    w_qkv,
    m_qkv,
    v_qkv,
    w_proj,
    m_proj,
    v_proj,
    w_fc1,
    m_fc1,
    v_fc1,
    w_fc2,
    m_fc2,
    v_fc2,
    split_bias,
    m_split,
    v_split,
    norm_bias,
    m_norm,
    v_norm,
):
    model_width = patches.shape[1]
    shard_width = w_qkv.shape[2]
    attn_scale = HD ** (-0.5)
    inputs = patches.astype(jnp.float32) + jnp.take(pos_table, visible.reshape(-1), axis=0)
    qkv_low, proj_low, fc1_low, fc2_low = (
        lax.all_gather(w_qkv.astype(jnp.bfloat16), "dp", axis=0, tiled=True),
        lax.all_gather(w_proj.astype(jnp.bfloat16), "dp", axis=1, tiled=True),
        lax.all_gather(w_fc1.astype(jnp.bfloat16), "dp", axis=0, tiled=True),
        lax.all_gather(w_fc2.astype(jnp.bfloat16), "dp", axis=2, tiled=True),
    )
    local_width = qkv_low.shape[2]
    heads_here = local_width // HD
    qkv_flat = qkv_low.reshape(model_width, 3 * local_width)
    fc1_flat = fc1_low.reshape(model_width, 4 * local_width)
    fc2_flat = fc2_low.reshape(4 * local_width, model_width)
    normed, norm_back = jax.vjp(layer_norm, inputs, norm_bias[0], norm_bias[1])
    normed_low = normed.astype(jnp.bfloat16)
    normed_full = lax.all_gather(normed_low, "tensor", axis=0, tiled=True)
    full_rows = normed_full.shape[0]
    head_shape = (full_rows // VISIBLE, VISIBLE, heads_here, HD)
    projected = jnp.dot(normed_full, qkv_flat, preferred_element_type=jnp.float32)
    queries = (projected[:, :local_width] + split_bias[0]).astype(jnp.bfloat16)
    keys_low = projected[:, local_width : 2 * local_width].astype(jnp.bfloat16)
    values_low = (projected[:, 2 * local_width :] + split_bias[1]).astype(jnp.bfloat16)
    query_heads = queries.reshape(head_shape)
    key_heads = keys_low.reshape(head_shape)
    value_heads = values_low.reshape(head_shape)
    scores = (
        jnp.einsum("bqhd,bkhd->bhqk", query_heads, key_heads, preferred_element_type=jnp.float32)
        * attn_scale
    )
    attention = jax.nn.softmax(scores, axis=-1)
    soft_low = attention.astype(jnp.bfloat16)
    mixed_low = (
        jnp.einsum("bhqk,bkhd->bqhd", soft_low, value_heads, preferred_element_type=jnp.float32)
        .reshape(full_rows, local_width)
        .astype(jnp.bfloat16)
    )
    attn_part = jnp.dot(mixed_low, proj_low, preferred_element_type=jnp.float32)
    attn_part = lax.psum_scatter(
        attn_part.astype(jnp.bfloat16), "tensor", scatter_dimension=0, tiled=True
    ).astype(jnp.float32)
    hidden_res = inputs + (attn_part + norm_bias[2])
    normed_two, norm_two_back = jax.vjp(layer_norm, hidden_res, norm_bias[3], norm_bias[4])
    normed_two_low = normed_two.astype(jnp.bfloat16)
    normed_two_full = lax.all_gather(normed_two_low, "tensor", axis=0, tiled=True)
    pre_gelu = jnp.dot(normed_two_full, fc1_flat, preferred_element_type=jnp.float32) + split_bias[
        2:
    ].reshape(-1)
    activated, gelu_back = jax.vjp(partial(jax.nn.gelu, approximate=False), pre_gelu)
    activated_low = activated.astype(jnp.bfloat16)
    ffn_part = jnp.dot(activated_low, fc2_flat, preferred_element_type=jnp.float32)
    ffn_part = lax.psum_scatter(
        ffn_part.astype(jnp.bfloat16), "tensor", scatter_dimension=0, tiled=True
    ).astype(jnp.float32)
    block_out = (hidden_res + (ffn_part + norm_bias[5])).astype(jnp.bfloat16)
    grad_out = cotangent.astype(jnp.float32)
    grad_ffn_full = lax.all_gather(cotangent, "tensor", axis=0, tiled=True)
    grad_fc2 = transpose_dot(activated_low, grad_ffn_full)
    grad_act = dot_back(grad_ffn_full, fc2_flat)
    grad_pre = gelu_back(grad_act)[0].astype(jnp.bfloat16)
    grad_fc1 = transpose_dot(normed_two_full, grad_pre)
    grad_fc1_bias = jnp.sum(grad_pre.astype(jnp.float32), axis=0).reshape(4, local_width)
    grad_normed_two = dot_back(grad_pre, fc1_flat)
    grad_normed_two = lax.psum_scatter(
        grad_normed_two.astype(jnp.bfloat16), "tensor", scatter_dimension=0, tiled=True
    ).astype(jnp.float32)
    grad_hidden_norm, grad_gain_two, grad_shift_two = norm_two_back(grad_normed_two)
    grad_hidden = grad_out + grad_hidden_norm
    grad_attn_low = grad_hidden.astype(jnp.bfloat16)
    grad_attn_full = lax.all_gather(grad_attn_low, "tensor", axis=0, tiled=True)
    grad_proj = transpose_dot(mixed_low, grad_attn_full)
    grad_mixed = dot_back(grad_attn_full, proj_low).astype(jnp.bfloat16).reshape(head_shape)
    grad_soft = jnp.einsum(
        "bqhd,bkhd->bhqk", grad_mixed, value_heads, preferred_element_type=jnp.float32
    )
    grad_values = jnp.einsum(
        "bhqk,bqhd->bkhd", soft_low, grad_mixed, preferred_element_type=jnp.float32
    ).astype(jnp.bfloat16)
    grad_scores = (
        attention * (grad_soft - jnp.sum(grad_soft * attention, axis=-1, keepdims=True))
    ).astype(jnp.bfloat16)
    grad_queries = (
        jnp.einsum("bhqk,bkhd->bqhd", grad_scores, key_heads, preferred_element_type=jnp.float32)
        * attn_scale
    ).astype(jnp.bfloat16)
    grad_keys = (
        jnp.einsum("bhqk,bqhd->bkhd", grad_scores, query_heads, preferred_element_type=jnp.float32)
        * attn_scale
    ).astype(jnp.bfloat16)
    grad_query_rows = grad_queries.reshape(full_rows, local_width)
    grad_value_rows = grad_values.reshape(full_rows, local_width)
    grad_proj_in = jnp.concatenate(
        [grad_query_rows, grad_keys.reshape(full_rows, local_width), grad_value_rows], axis=1
    )
    grad_qkv = transpose_dot(normed_full, grad_proj_in).reshape(model_width, 3, local_width)
    grad_normed = dot_back(grad_proj_in, qkv_flat)
    grad_normed = lax.psum_scatter(
        grad_normed.astype(jnp.bfloat16), "tensor", scatter_dimension=0, tiled=True
    ).astype(jnp.float32)
    grad_input_norm, grad_gain_one, grad_shift_one = norm_back(grad_normed)
    input_grad = grad_hidden + grad_input_norm
    grad_split = jnp.concatenate(
        [
            jnp.sum(grad_query_rows.astype(jnp.float32), axis=0)[None, :],
            jnp.sum(grad_value_rows.astype(jnp.float32), axis=0)[None, :],
            grad_fc1_bias,
        ],
        axis=0,
    )
    grad_norm_rows = jnp.stack(
        [
            grad_gain_one,
            grad_shift_one,
            jnp.sum(grad_attn_low.astype(jnp.float32), axis=0),
            grad_gain_two,
            grad_shift_two,
            jnp.sum(grad_out, axis=0),
        ]
    )
    grad_fc1 = grad_fc1.reshape(model_width, 4, local_width)
    grad_fc2 = grad_fc2.reshape(4, local_width, model_width)
    shards = (
        lax.psum_scatter(grad_qkv, "dp", scatter_dimension=0, tiled=True),
        lax.psum_scatter(grad_proj, "dp", scatter_dimension=1, tiled=True),
        lax.psum_scatter(grad_fc1, "dp", scatter_dimension=0, tiled=True),
        lax.psum_scatter(grad_fc2, "dp", scatter_dimension=2, tiled=True),
    )
    pair_start = lax.axis_index("tensor") * shard_width
    split_padded = lax.dynamic_update_slice_in_dim(
        jnp.zeros((6, model_width), jnp.float32), grad_split, pair_start, 1
    )
    local_square = square_sum(shards)
    norm_total, split_whole, square_total = lax.psum(
        (grad_norm_rows, split_padded, local_square), ("dp", "tensor")
    )
    split_total = lax.dynamic_slice_in_dim(split_whole, pair_start, shard_width, 1)
    grad_norm = jnp.sqrt(
        square_total + jnp.sum(norm_total * norm_total) + jnp.sum(split_whole * split_whole)
    )
    factor = jnp.minimum(1.0, clip_value / (grad_norm + 1e-06))
    step_value = step_count[0].astype(jnp.float32)
    bias_first = 1.0 - jnp.power(beta_one, step_value)
    bias_second = 1.0 - jnp.power(beta_two, step_value)
    qkv_out = adam_update(
        w_qkv, shards[0], m_qkv, v_qkv, factor, bias_first, bias_second, matrix_rate, matrix_decay
    )
    proj_out = adam_update(
        w_proj, shards[1], m_proj, v_proj, factor, bias_first, bias_second, proj_rate, matrix_decay
    )
    fc1_out = adam_update(
        w_fc1, shards[2], m_fc1, v_fc1, factor, bias_first, bias_second, matrix_rate, matrix_decay
    )
    fc2_out = adam_update(
        w_fc2, shards[3], m_fc2, v_fc2, factor, bias_first, bias_second, matrix_rate, matrix_decay
    )
    split_out = adam_update(
        split_bias, split_total, m_split, v_split, factor, bias_first, bias_second, vector_rate, 0.0
    )
    norm_out = adam_update(
        norm_bias, norm_total, m_norm, v_norm, factor, bias_first, bias_second, vector_rate, 0.0
    )
    return (
        block_out,
        input_grad,
        grad_norm,
        qkv_out[0],
        qkv_out[1],
        qkv_out[2],
        proj_out[0],
        proj_out[1],
        proj_out[2],
        fc1_out[0],
        fc1_out[1],
        fc1_out[2],
        fc2_out[0],
        fc2_out[1],
        fc2_out[2],
        split_out[0],
        split_out[1],
        split_out[2],
        norm_out[0],
        norm_out[1],
        norm_out[2],
    )


def solution(mesh):
    return jax.shard_map(
        body,
        mesh=mesh,
        in_specs=(
            P(("dp", "tensor"), None),
            P(("dp", "tensor"), None),
            P(),
            P(("dp", "tensor"), None),
            P(),
            P("dp", None, "tensor"),
            P("dp", None, "tensor"),
            P("dp", None, "tensor"),
            P("tensor", "dp"),
            P("tensor", "dp"),
            P("tensor", "dp"),
            P("dp", None, "tensor"),
            P("dp", None, "tensor"),
            P("dp", None, "tensor"),
            P(None, "tensor", "dp"),
            P(None, "tensor", "dp"),
            P(None, "tensor", "dp"),
            P(None, "tensor"),
            P(None, "tensor"),
            P(None, "tensor"),
            P(),
            P(),
            P(),
        ),
        out_specs=(
            P(("dp", "tensor"), None),
            P(("dp", "tensor"), None),
            P(),
            P("dp", None, "tensor"),
            P("dp", None, "tensor"),
            P("dp", None, "tensor"),
            P("tensor", "dp"),
            P("tensor", "dp"),
            P("tensor", "dp"),
            P("dp", None, "tensor"),
            P("dp", None, "tensor"),
            P("dp", None, "tensor"),
            P(None, "tensor", "dp"),
            P(None, "tensor", "dp"),
            P(None, "tensor", "dp"),
            P(None, "tensor"),
            P(None, "tensor"),
            P(None, "tensor"),
            P(),
            P(),
            P(),
        ),
        check_vma=False,
    )
```

profile of v0, /device:TPU:0, one launch (start us, length us, event | category | flops | bytes accessed | tf_op | source)
XLA Modules:
  0.0 1264.1 jit_solution(11873003725389010654)
XLA Ops:
  25.4 26.5 %all_gather.26 = bf16[384,768]{0,1:T(8,128)(2,1)} all-gather(bf16[384,48]{0,1:T(8,128)(2,1)S(1)} %convert_element_type.130), channel_id=1, replica_groups=mesh['dp'=16,'tensor'=2] {'dp'}, dimensions={1}, use_global_device_ids=true | all-gather | bytes 626688 | tf_op jit(solution)/shard_map/all_gather | solution.py:90
  57.4 63.3 %all-gather.8.cloned.1.call-done = bf16[3136,768]{1,0:T(8,128)(2,1)} async-done(((bf16[1568,768]{1,0:T(8,128)(2,1)}), bf16[3136,768]{1,0:T(8,128)(2,1)}) %all-gather.8.cloned.1.call-update) | async-done | bytes 4816912 | tf_op jit(solution)/shard_map/all_gather | solution.py:101
  147.2 11.9 fusion.29
  159.0 14.7 %fusion.70 = (f32[64,6,49]{2,1,0:T(8,128)S(1)}, f32[64,6,49,49]{2,3,1,0:T(8,128)}) fusion(f32[64,6,49,49]{2,3,1,0:T(8,128)} %fusion.29), kind=kOutput, calls=%fused_computation.156 | output fusion | flops 3687984 | bytes 7451136 | tf_op jit(solution)/shard_map/sub | solution.py:115
  216.1 59.5 %reduce-scatter.7.cloned.1.call-done = bf16[1568,768]{1,0:T(8,128)(2,1)} async-done(((bf16[3136,768]{1,0:T(8,128)(2,1)}), bf16[1568,768]{1,0:T(8,128)(2,1)}) %reduce-scatter.7.cloned.1.call-update) | async-done | bytes 2408464 | tf_op jit(solution)/shard_map/reduce_scatter | solution.py:123
  284.6 36.1 %all-gather.14.cloned.1.call-done = bf16[768,4,384]{2,1,0:T(4,128)(2,1)} async-done(((bf16[48,4,384]{2,1,0:T(4,128)(2,1)}), bf16[768,4,384]{2,1,0:T(4,128)(2,1)}) %all-gather.14.cloned.1.call-update) | async-done | bytes 2359312 | tf_op jit(solution)/shard_map/all_gather | solution.py:91
  324.2 40.3 %all-gather.16.cloned.1.call-done = bf16[4,384,768]{1,0,2:T(4,128)(2,1)} async-done(((bf16[4,384,48]{1,0,2:T(4,128)(2,1)}), bf16[4,384,768]{1,0,2:T(4,128)(2,1)}) %all-gather.16.cloned.1.call-update) | async-done | bytes 2359312 | tf_op jit(solution)/shard_map/all_gather | solution.py:92
  368.6 60.3 %all-gather.12.cloned.1.call-done = bf16[3136,768]{1,0:T(8,128)(2,1)} async-done(((bf16[1568,768]{1,0:T(8,128)(2,1)}), bf16[3136,768]{1,0:T(8,128)(2,1)}) %all-gather.12.cloned.1.call-update) | async-done | bytes 4816912 | tf_op jit(solution)/shard_map/all_gather | solution.py:129
  428.9 51.0 %multiply_convert_fusion = (bf16[3136,1536]{1,0:T(8,128)(2,1)}, f32[3136,1536]{1,0:T(8,128)}, f32[3136,1536]{1,0:T(8,128)}) fusion(f32[1536]{0:T(1024)S(1)} %add.283, bf16[3136,768]{1,0:T(8,128)(2,1)} %all-gather.12.cloned.1.call-done, bf16[768,1536]{1,0:T(8,128)(2,1)} %bitcast.64), kind=kOutput, calls=%fused_computation.6 | convolution fusion | flops 7716667392 | bytes 55351296 | tf_op jit(solution)/shard_map/dot_general | solution.py:130
  479.9 14.3 %all-gather.18.cloned.1.call-done = bf16[3136,768]{1,0:T(8,128)(2,1)} async-done(((bf16[1568,768]{1,0:T(8,128)(2,1)}), bf16[3136,768]{1,0:T(8,128)(2,1)}) %all-gather.18.cloned.1.call-update) | async-done | bytes 4816912 | tf_op jit(solution)/shard_map/all_gather | solution.py:141
  494.2 24.2 %convert_reduce_fusion = (f32[1536]{0:T(1024)}, bf16[3136,1536]{1,0:T(8,128)(2,1)}) fusion(f32[3136,1536]{1,0:T(8,128)} %get-tuple-element.108, f32[3136,1536]{1,0:T(8,128)} %get-tuple-element.120, bf16[3136,768]{1,0:T(8,128)(2,1)} %all-gather.18.cloned.1.call-done, bf16[1536,768]{1,0:T(8,128)(2,1)S(1)} %bitcast.62), kind=kOutput, calls=%fused_computation.4 | convolution fusion | flops 7475821056 | bytes 55351296 | tf_op jit(solution)/shard_map/dot_general | solution.py:47
  518.5 13.5 %convolution_convert_fusion.2 = bf16[3136,768]{1,0:T(8,128)(2,1)} fusion(bf16[3136,1536]{1,0:T(8,128)(2,1)} %get-tuple-element.124, bf16[768,1536]{1,0:T(8,128)(2,1)S(1)} %bitcast.65), kind=kOutput, calls=%fused_computation.40 | convolution fusion | flops 7401160704 | bytes 16809984 | tf_op jit(solution)/shard_map/dot_general | solution.py:47
  532.1 13.0 %convolution_convert_fusion.3 = bf16[3136,768]{1,0:T(8,128)(2,1)} fusion(bf16[3136,1536]{1,0:T(8,128)(2,1)} %get-tuple-element.107, bf16[1536,768]{1,0:T(8,128)(2,1)S(1)} %bitcast.63), kind=kOutput, calls=%fused_computation.41 | convolution fusion | flops 7401160704 | bytes 16809984 | tf_op jit(solution)/shard_map/dot_general | solution.py:135
  545.2 48.1 %reduce-scatter.11.cloned.1.call-done = bf16[1568,768]{1,0:T(8,128)(2,1)} async-done(((bf16[3136,768]{1,0:T(8,128)(2,1)}), bf16[1568,768]{1,0:T(8,128)(2,1)}) %reduce-scatter.11.cloned.1.call-update) | async-done | bytes 2408464 | tf_op jit(solution)/shard_map/reduce_scatter | solution.py:148
  598.3 58.5 %reduce-scatter.9.cloned.1.call-done = bf16[1568,768]{1,0:T(8,128)(2,1)} async-done(((bf16[3136,768]{1,0:T(8,128)(2,1)}), bf16[1568,768]{1,0:T(8,128)(2,1)}) %reduce-scatter.9.cloned.1.call-update) | async-done | bytes 2408464 | tf_op jit(solution)/shard_map/reduce_scatter | solution.py:136
  668.9 13.9 %fusion.73 = f32[768,1536]{1,0:T(8,128)} fusion(bf16[3136,768]{1,0:T(8,128)(2,1)} %all-gather.12.cloned.1.call-done, bf16[3136,1536]{1,0:T(8,128)(2,1)} %get-tuple-element.124), kind=kOutput, calls=%fused_computation.159 | convolution fusion | flops 7398752256 | bytes 19169280 | tf_op jit(solution)/shard_map/dot_general | solution.py:41
  689.1 13.7 %fusion.74 = f32[1536,768]{1,0:T(8,128)} fusion(bf16[3136,1536]{1,0:T(8,128)(2,1)} %get-tuple-element.107, bf16[3136,768]{1,0:T(8,128)(2,1)} %all-gather.18.cloned.1.call-done), kind=kOutput, calls=%fused_computation.160 | convolution fusion | flops 7398752256 | bytes 19169280 | tf_op jit(solution)/shard_map/dot_general | solution.py:41
  709.0 23.8 %all-gather.20.cloned.1.call-done = bf16[3136,768]{1,0:T(8,128)(2,1)} async-done(((bf16[1568,768]{1,0:T(8,128)(2,1)}), bf16[3136,768]{1,0:T(8,128)(2,1)}) %all-gather.20.cloned.1.call-update) | async-done | bytes 4816912 | tf_op jit(solution)/shard_map/all_gather | solution.py:154
  778.8 14.2 %multiply_reduce_fusion = (f32[64,6,49]{2,1,0:T(8,128)S(1)}, f32[64,6,49,49]{2,3,1,0:T(8,128)}) fusion(f32[64,6,49,49]{2,3,1,0:T(8,128)} %get-tuple-element.119, f32[64,6,49]{2,1,0:T(8,128)S(1)} %copy-done.19, bf16[64,49,6,64]{3,2,1,0:T(8,128)(2,1)} %reshape.240, bf16[64,49,6,64]{3,2,1,0:T(8,128)(2,1)} %reshape.243), kind=kOutput, calls=%fused_computation.26 | convolution fusion | flops 120761088 | bytes 12343296 | tf_op jit(solution)/shard_map/bqhd,bkhd->bhqk/dot_general | solution.py:157
  894.5 11.3 convolution_convert_fusion.1
  911.5 23.7 %reduce-scatter.15.cloned.1.call-done = f32[384,48]{0,1:T(8,128)} async-done(((f32[384,768]{0,1:T(8,128)}), f32[384,48]{0,1:T(8,128)}) %reduce-scatter.15.cloned.1.call-update) | async-done | bytes 73744 | tf_op jit(solution)/shard_map/reduce_scatter | solution.py:208
  936.7 186.0 %all-reduce.6.cloned.1.call-done = (f32[768,3,384]{2,1,0:T(4,128)}, f32[768,4,384]{2,1,0:T(4,128)}) async-done(((f32[768,3,384]{2,1,0:T(4,128)}, f32[768,4,384]{2,1,0:T(4,128)}), (f32[768,3,384]{2,1,0:T(4,128)}, f32[768,4,384]{2,1,0:T(4,128)})) %all-reduce.6.cloned.1.call-update) | async-done | bytes 8257552
  1129.4 56.7 %reduce-scatter.13.cloned.1.call-done = bf16[1568,768]{1,0:T(8,128)(2,1)} async-done(((bf16[3136,768]{1,0:T(8,128)(2,1)}), bf16[1568,768]{1,0:T(8,128)(2,1)}) %reduce-scatter.13.cloned.1.call-update) | async-done | bytes 2408464 | tf_op jit(solution)/shard_map/reduce_scatter | solution.py:181
  1203.3 40.0 %all-reduce.2 = (f32[]{:T(128)}, f32[6,768]{1,0:T(8,128)S(1)}, f32[6,768]{1,0:T(8,128)S(1)}) all-reduce(f32[]{:T(128)S(6)} %add.294, f32[6,768]{1,0:T(8,128)S(1)} %stack.15, f32[6,768]{1,0:T(8,128)} %copy-done.37), channel_id=1, replica_groups=mesh['dp'=16,'tensor'=2] {'dp','tensor'}, use_global_device_ids=true, to_apply=%region_23.24 | all-reduce | flops 9217 | bytes 73736 | tf_op jit(solution)/shard_map/psum | solution.py:217
  (227 shorter events, 323.6 us)
Async XLA Ops:
  7.2 47.6 %all-gather.10.cloned.1.call-start = ((), (), s32[]{:S(2)}) async-start(), calls=%async_computation.7 | async-start | bytes 1880064 | tf_op jit(solution)/shard_map/all_gather | solution.py:89
  8.9 111.8 %all-gather.8.cloned.1.call-start = ((), (), s32[]{:S(2)}) async-start(), calls=%async_computation.6 | async-start | bytes 7225344 | tf_op jit(solution)/shard_map/all_gather | solution.py:101
  17.5 262.8 %copy-start.47 = (f32[768]{0:T(1024)}, f32[768]{0:T(1024)S(1)}, u32[]{:S(2)}) copy-start(f32[768]{0:T(1024)S(1)} %get-tuple-element.72) | copy-start | bytes 9220
  25.3 250.3 %reduce-scatter.7.cloned.1.call-start = ((), (), s32[]{:S(2)}) async-start(), calls=%async_computation.8 | async-start | bytes 7225344 | tf_op jit(solution)/shard_map/reduce_scatter | solution.py:123
  57.4 63.3 %copy-start.14 = (bf16[768,3,384]{0,2,1:T(8,128)(2,1)}, bf16[768,3,384]{0,2,1:T(8,128)(2,1)S(1)}, u32[]{:S(2)}) copy-start(bf16[768,3,384]{0,2,1:T(8,128)(2,1)S(1)} %copy.116) | copy-start | bytes 5308420
  214.3 106.3 %all-gather.14.cloned.1.call-start = ((), (), s32[]{:S(2)}) async-start(), calls=%async_computation.10 | async-start | bytes 2506752 | tf_op jit(solution)/shard_map/all_gather | solution.py:91
  215.1 149.3 %all-gather.16.cloned.1.call-start = ((), (), s32[]{:S(2)}) async-start(), calls=%async_computation.11 | async-start | bytes 2506752 | tf_op jit(solution)/shard_map/all_gather | solution.py:92
  216.1 212.8 %all-gather.12.cloned.1.call-start = ((), (), s32[]{:S(2)}) async-start(), calls=%async_computation.9 | async-start | bytes 7225344 | tf_op jit(solution)/shard_map/all_gather | solution.py:129
  283.8 210.5 %all-gather.18.cloned.1.call-start = ((), (), s32[]{:S(2)}) async-start(), calls=%async_computation.13 | async-start | bytes 7225344 | tf_op jit(solution)/shard_map/all_gather | solution.py:141
  284.5 308.8 %reduce-scatter.11.cloned.1.call-start = ((), (), s32[]{:S(2)}) async-start(), calls=%async_computation.14 | async-start | bytes 7225344 | tf_op jit(solution)/shard_map/reduce_scatter | solution.py:148
  532.0 124.8 %reduce-scatter.9.cloned.1.call-start = ((), (), s32[]{:S(2)}) async-start(), calls=%async_computation.12 | async-start | bytes 7225344 | tf_op jit(solution)/shard_map/reduce_scatter | solution.py:136
  532.1 61.2 %copy-start.29 = (f32[1568]{0:T(1024)S(1)}, f32[1568]{0:T(1024)}, u32[]{:S(2)}) copy-start(f32[1568]{0:T(1024)} %copy-done.28) | copy-start | bytes 18820
  532.1 61.2 %copy-start.31 = (f32[1568]{0:T(1024)S(1)}, f32[1568]{0:T(1024)}, u32[]{:S(2)}) copy-start(f32[1568]{0:T(1024)} %copy-done.30) | copy-start | bytes 18820
  545.1 111.6 %copy-start.50 = (f32[768]{0:T(1024)S(1)}, f32[768]{0:T(1024)}, u32[]{:S(2)}) copy-start(f32[768]{0:T(1024)} %get-tuple-element.70) | copy-start | bytes 9220
  545.2 187.6 %all-gather.20.cloned.1.call-start = ((), (), s32[]{:S(2)}) async-start(), calls=%async_computation.15 | async-start | bytes 7225344 | tf_op jit(solution)/shard_map/all_gather | solution.py:154
  668.9 239.1 %reduce-scatter.17.cloned.1.call-start = ((), (), s32[]{:S(2)}) async-start(), calls=%async_computation.18 | async-start | bytes 5013504 | tf_op jit(solution)/shard_map/reduce_scatter | solution.py:210
  708.9 226.3 %reduce-scatter.15.cloned.1.call-start = ((), (), s32[]{:S(2)}) async-start(), calls=%async_computation.17 | async-start | bytes 1253376 | tf_op jit(solution)/shard_map/reduce_scatter | solution.py:208
  877.0 245.7 %all-reduce.6.cloned.1.call-start = ((), (), s32[]{:S(2)}) async-start(), calls=%async_computation.19 | async-start | bytes 18874368
  894.5 291.7 %reduce-scatter.13.cloned.1.call-start = ((), (), s32[]{:S(2)}) async-start(), calls=%async_computation.16 | async-start | bytes 7225344 | tf_op jit(solution)/shard_map/reduce_scatter | solution.py:181
  905.8 280.3 %copy-start.27 = (f32[1568]{0:T(1024)S(1)}, f32[1568]{0:T(1024)}, u32[]{:S(2)}) copy-start(f32[1568]{0:T(1024)} %copy-done.26) | copy-start | bytes 18820
  905.8 280.3 %copy-start.35 = (f32[768]{0:T(1024)S(1)}, f32[768]{0:T(1024)}, u32[]{:S(2)}) copy-start(f32[768]{0:T(1024)} %copy-done.34) | copy-start | bytes 9220
  905.9 285.1 %copy-start.42 = (f32[1568]{0:T(1024)S(1)}, f32[1568]{0:T(1024)}, u32[]{:S(2)}) copy-start(f32[1568]{0:T(1024)} %copy-done.41) | copy-start | bytes 18820
  905.9 285.1 %copy-start.33 = (f32[1568]{0:T(1024)S(1)}, f32[1568]{0:T(1024)}, u32[]{:S(2)}) copy-start(f32[1568]{0:T(1024)} %copy-done.32) | copy-start | bytes 18820
  911.5 284.3 %copy-start.37 = (f32[6,768]{1,0:T(8,128)}, f32[6,768]{1,0:T(8,128)S(1)}, u32[]{:S(2)}) copy-start(f32[6,768]{1,0:T(8,128)S(1)} %maximum_dynamic-update-slice_fusion) | copy-start | bytes 55300
  (43 other events, 737.9 us)
Sparse Core Ops, SparseCore 0:
  10.9 43.8 all-gather.9
  56.9 63.7 all-gather.7
  214.5 61.1 reduce-scatter.6
  278.3 42.3 all-gather.13
  323.4 41.0 all-gather.15
  366.4 62.4 all-gather.11
  430.4 63.7 all-gather.17
  532.1 61.1 reduce-scatter.10
  595.6 61.1 reduce-scatter.8
  669.0 63.7 all-gather.19
  736.6 75.5 reduce-scatter.16
  877.2 58.0 reduce-scatter.14
  939.0 183.7 all-reduce.5
  1124.9 61.2 reduce-scatter.12
where the time goes:
time: 1270 us; the launch traced here: 1260 us
  waiting for transfers between devices  674 us (53%)
  matrix products  246 us (19%)
  local copies, waits for them, and re-layouts  162 us (13%)
  other arithmetic  93.1 us (7%)
  blocking collectives  66.5 us (5%)
  between operations  22 us (2%)
    unnamed x15, waiting for transfers between devices  187 us
    all_gather x1, waiting for transfers between devices, body(): normed_full = lax.all_gather(normed_low, 'tensor', axis=0, tiled=True)  63.3 us
    all_gather x1, waiting for transfers between devices, body(): lax.all_gather(normed_two_low, 'tensor', axis=0, tiled=True)  60.3 us
    reduce_scatter x1, waiting for transfers between devices, body(): lax.psum_scatter(attn_part.astype(jnp.bfloat16), 'tensor', scatter_dimens...  59.5 us
    reduce_scatter x1, waiting for transfers between devices, body(): lax.psum_scatter(ffn_part.astype(jnp.bfloat16), 'tensor', scatter_dimensi...  58.5 us
    reduce_scatter x1, waiting for transfers between devices, body(): lax.psum_scatter(grad_normed.astype(jnp.bfloat16), 'tensor', scatter_dime...  56.7 us
    dot_general x4, matrix products, dot_back(): lax.dot_general(left_side, right_side, (((1,), (1,)), ((), ())), preferre...  55.5 us
    dot_general x1, matrix products, body(): jnp.dot(normed_two_full, fc1_flat, preferred_element_type=jnp.float32)  51 us
  transfers between devices with their start and end apart: 14, of which 13 were waited for; matrix products, arithmetic and copies ran while one was open for 25% of the time, Pallas kernels for 0%

commit v1 on v0

v1 whole, which is shorter than its diff:
```python
import jax
import jax.numpy as jnp
from jax import lax
from jax.sharding import PartitionSpec as P

HD = 64
VISIBLE = 49


norm_eps = 1e-06
beta_one = 0.9
beta_two = 0.95
adam_eps = 1e-08
clip_value = 1.0
matrix_rate = 0.02
proj_rate = 0.08
vector_rate = 0.2
matrix_decay = 0.05


def layer_norm(values, row_gain, row_shift):
    row_mean = jnp.mean(values, axis=-1, keepdims=True)
    centred = values - row_mean
    variance = jnp.mean(centred * centred, axis=-1, keepdims=True)
    return centred * lax.rsqrt(variance + norm_eps) * row_gain + row_shift


def adam_update(
    weight, gradient, first_moment, second, factor, bias_first, bias_second, learn_rate, decay_rate
):
    clipped = gradient * factor
    first_new = beta_one * first_moment + (1.0 - beta_one) * clipped
    second_new = beta_two * second + (1.0 - beta_two) * clipped * clipped
    direction = first_new / bias_first / (jnp.sqrt(second_new / bias_second) + adam_eps)
    return (weight - learn_rate * (direction + decay_rate * weight), first_new, second_new)


def transpose_dot(left_side, right_side):
    return lax.dot_general(
        left_side, right_side, (((0,), (0,)), ((), ())), preferred_element_type=jnp.float32
    )


def dot_back(left_side, right_side):
    return lax.dot_general(
        left_side, right_side, (((1,), (1,)), ((), ())), preferred_element_type=jnp.float32
    )


def square_sum(arrays):
    total = jnp.sum(arrays[0] * arrays[0])
    for member in arrays[1:]:
        total = total + jnp.sum(member * member)
    return total


def standard_normal(values):
    cumulative = 0.5 + 0.5 * lax.erf(values * (0.5**0.5))
    density = jnp.exp(-0.5 * values * values) * (0.5 / jnp.pi) ** 0.5
    return cumulative, density


def body(
    patches,
    visible,
    pos_table,
    cotangent,
    step_count,
    w_qkv,
    m_qkv,
    v_qkv,
    w_proj,
    m_proj,
    v_proj,
    w_fc1,
    m_fc1,
    v_fc1,
    w_fc2,
    m_fc2,
    v_fc2,
    split_bias,
    m_split,
    v_split,
    norm_bias,
    m_norm,
    v_norm,
):
    model_width = patches.shape[1]
    shard_rows = w_qkv.shape[0]
    shard_width = w_qkv.shape[2]
    halves = model_width // shard_width
    attn_scale = HD ** (-0.5)
    full_rows = patches.shape[0]
    every = ("tensor", "dp")
    low_type = jnp.bfloat16

    def rows_of(proj_like):
        return jnp.swapaxes(proj_like, -1, -2)

    def gather(block):
        whole = lax.all_gather(block.astype(low_type), every, axis=0, tiled=True)
        return whole.reshape(halves, model_width, block.shape[1])

    fc2_rows = jnp.transpose(w_fc2, (2, 0, 1)).reshape(shard_rows, 4 * shard_width)
    qkv_low = gather(w_qkv.reshape(shard_rows, 3 * shard_width))
    rest_low = gather(
        jnp.concatenate(
            [rows_of(w_proj), w_fc1.reshape(shard_rows, 4 * shard_width), fc2_rows], axis=1
        )
    )
    proj_low = [rest_low[t, :, :shard_width] for t in range(halves)]
    fc1_low = [rest_low[t, :, shard_width : 5 * shard_width] for t in range(halves)]
    fc2_low = [rest_low[t, :, 5 * shard_width :] for t in range(halves)]
    split_whole_bias = lax.all_gather(split_bias, "tensor", axis=0, tiled=False)

    inputs = patches.astype(jnp.float32) + jnp.take(pos_table, visible.reshape(-1), axis=0)
    normed, norm_back = jax.vjp(layer_norm, inputs, norm_bias[0], norm_bias[1])
    normed_low = normed.astype(low_type)
    heads_here = shard_width // HD
    head_shape = (full_rows // VISIBLE, VISIBLE, heads_here, HD)
    attended = jnp.zeros((full_rows, model_width), jnp.float32)
    kept = []
    for t in range(halves):
        projected = jnp.dot(normed_low, qkv_low[t], preferred_element_type=jnp.float32)
        bias_t = split_whole_bias[t]
        query_heads = (projected[:, :shard_width] + bias_t[0]).astype(low_type).reshape(head_shape)
        key_heads = projected[:, shard_width : 2 * shard_width].astype(low_type).reshape(head_shape)
        value_heads = (
            (projected[:, 2 * shard_width :] + bias_t[1]).astype(low_type).reshape(head_shape)
        )
        scores = (
            jnp.einsum(
                "bqhd,bkhd->bhqk", query_heads, key_heads, preferred_element_type=jnp.float32
            )
            * attn_scale
        )
        attention = jax.nn.softmax(scores, axis=-1)
        soft_low = attention.astype(low_type)
        mixed_low = (
            jnp.einsum(
                "bhqk,bkhd->bqhd", soft_low, value_heads, preferred_element_type=jnp.float32
            )
            .reshape(full_rows, shard_width)
            .astype(low_type)
        )
        attended = attended + dot_back(mixed_low, proj_low[t])
        kept.append((query_heads, key_heads, value_heads, attention, soft_low, mixed_low))
    hidden_res = inputs + (attended + norm_bias[2])
    normed_two, norm_two_back = jax.vjp(layer_norm, hidden_res, norm_bias[3], norm_bias[4])
    normed_two_low = normed_two.astype(low_type)
    ffn_out = jnp.zeros((full_rows, model_width), jnp.float32)
    grad_out = cotangent.astype(jnp.float32)
    grad_normed_two = jnp.zeros((full_rows, model_width), jnp.float32)
    grad_fc1, grad_fc2, grad_fc1_bias = [], [], []
    for t in range(halves):
        pre_gelu = jnp.dot(
            normed_two_low, fc1_low[t], preferred_element_type=jnp.float32
        ) + split_whole_bias[t, 2:].reshape(-1)
        cumulative, density = standard_normal(pre_gelu)
        activated_low = (pre_gelu * cumulative).astype(low_type)
        slope_low = (cumulative + pre_gelu * density).astype(low_type)
        ffn_out = ffn_out + dot_back(activated_low, fc2_low[t])
        grad_fc2.append(transpose_dot(cotangent, activated_low).astype(low_type))
        grad_act = jnp.dot(cotangent, fc2_low[t], preferred_element_type=jnp.float32)
        grad_pre = (grad_act * slope_low.astype(jnp.float32)).astype(low_type)
        grad_fc1.append(transpose_dot(normed_two_low, grad_pre).astype(low_type))
        grad_fc1_bias.append(jnp.sum(grad_pre.astype(jnp.float32), axis=0).reshape(4, shard_width))
        grad_normed_two = grad_normed_two + dot_back(grad_pre, fc1_low[t])
    block_out = (hidden_res + (ffn_out + norm_bias[5])).astype(low_type)

    def scatter(parts):
        stacked = jnp.stack(parts).reshape(halves * model_width, parts[0].shape[1])
        return lax.psum_scatter(stacked, every, scatter_dimension=0, tiled=True).astype(jnp.float32)

    ffn_shard = scatter(
        [jnp.concatenate([grad_fc1[t], grad_fc2[t]], axis=1) for t in range(halves)]
    )
    grad_hidden_norm, grad_gain_two, grad_shift_two = norm_two_back(grad_normed_two)
    grad_hidden = grad_out + grad_hidden_norm
    grad_attn_low = grad_hidden.astype(low_type)
    grad_normed = jnp.zeros((full_rows, model_width), jnp.float32)
    grad_front, grad_query_bias = [], []
    for t in range(halves):
        query_heads, key_heads, value_heads, attention, soft_low, mixed_low = kept[t]
        grad_proj = transpose_dot(grad_attn_low, mixed_low).astype(low_type)
        grad_mixed = (
            jnp.dot(grad_attn_low, proj_low[t], preferred_element_type=jnp.float32)
            .astype(low_type)
            .reshape(head_shape)
        )
        grad_soft = jnp.einsum(
            "bqhd,bkhd->bhqk", grad_mixed, value_heads, preferred_element_type=jnp.float32
        )
        grad_values = jnp.einsum(
            "bhqk,bqhd->bkhd", soft_low, grad_mixed, preferred_element_type=jnp.float32
        ).astype(low_type)
        grad_scores = (
            attention * (grad_soft - jnp.sum(grad_soft * attention, axis=-1, keepdims=True))
        ).astype(low_type)
        grad_queries = (
            jnp.einsum(
                "bhqk,bkhd->bqhd", grad_scores, key_heads, preferred_element_type=jnp.float32
            )
            * attn_scale
        ).astype(low_type)
        grad_keys = (
            jnp.einsum(
                "bhqk,bqhd->bkhd", grad_scores, query_heads, preferred_element_type=jnp.float32
            )
            * attn_scale
        ).astype(low_type)
        grad_query_rows = grad_queries.reshape(full_rows, shard_width)
        grad_value_rows = grad_values.reshape(full_rows, shard_width)
        grad_proj_in = jnp.concatenate(
            [grad_query_rows, grad_keys.reshape(full_rows, shard_width), grad_value_rows], axis=1
        )
        grad_qkv = transpose_dot(normed_low, grad_proj_in).astype(low_type)
        grad_front.append(jnp.concatenate([grad_qkv, grad_proj], axis=1))
        grad_normed = grad_normed + dot_back(grad_proj_in, qkv_low[t])
        grad_query_bias.append(
            jnp.stack(
                [
                    jnp.sum(grad_query_rows.astype(jnp.float32), axis=0),
                    jnp.sum(grad_value_rows.astype(jnp.float32), axis=0),
                ]
            )
        )
    front_shard = scatter(grad_front)
    grad_input_norm, grad_gain_one, grad_shift_one = norm_back(grad_normed)
    input_grad = grad_hidden + grad_input_norm
    grad_split = jnp.stack(
        [jnp.concatenate([grad_query_bias[t], grad_fc1_bias[t]]) for t in range(halves)]
    )
    grad_norm_rows = jnp.stack(
        [
            grad_gain_one,
            grad_shift_one,
            jnp.sum(grad_attn_low.astype(jnp.float32), axis=0),
            grad_gain_two,
            grad_shift_two,
            jnp.sum(grad_out, axis=0),
        ]
    )
    shards = (
        front_shard[:, : 3 * shard_width].reshape(shard_rows, 3, shard_width),
        rows_of(front_shard[:, 3 * shard_width :]),
        ffn_shard[:, : 4 * shard_width].reshape(shard_rows, 4, shard_width),
        jnp.transpose(
            ffn_shard[:, 4 * shard_width :].reshape(shard_rows, 4, shard_width), (1, 2, 0)
        ),
    )
    local_square = square_sum((front_shard, ffn_shard))
    norm_total, split_whole, square_total = lax.psum(
        (grad_norm_rows, grad_split, local_square), ("dp", "tensor")
    )
    split_total = split_whole[lax.axis_index("tensor")]
    grad_norm = jnp.sqrt(
        square_total + jnp.sum(norm_total * norm_total) + jnp.sum(split_whole * split_whole)
    )
    factor = jnp.minimum(1.0, clip_value / (grad_norm + 1e-06))
    step_value = step_count[0].astype(jnp.float32)
    bias_first = 1.0 - jnp.power(beta_one, step_value)
    bias_second = 1.0 - jnp.power(beta_two, step_value)
    qkv_out = adam_update(
        w_qkv, shards[0], m_qkv, v_qkv, factor, bias_first, bias_second, matrix_rate, matrix_decay
    )
    proj_out = adam_update(
        w_proj, shards[1], m_proj, v_proj, factor, bias_first, bias_second, proj_rate, matrix_decay
    )
    fc1_out = adam_update(
        w_fc1, shards[2], m_fc1, v_fc1, factor, bias_first, bias_second, matrix_rate, matrix_decay
    )
    fc2_out = adam_update(
        w_fc2, shards[3], m_fc2, v_fc2, factor, bias_first, bias_second, matrix_rate, matrix_decay
    )
    split_out = adam_update(
        split_bias, split_total, m_split, v_split, factor, bias_first, bias_second, vector_rate, 0.0
    )
    norm_out = adam_update(
        norm_bias, norm_total, m_norm, v_norm, factor, bias_first, bias_second, vector_rate, 0.0
    )
    return (
        block_out,
        input_grad,
        grad_norm,
        qkv_out[0],
        qkv_out[1],
        qkv_out[2],
        proj_out[0],
        proj_out[1],
        proj_out[2],
        fc1_out[0],
        fc1_out[1],
        fc1_out[2],
        fc2_out[0],
        fc2_out[1],
        fc2_out[2],
        split_out[0],
        split_out[1],
        split_out[2],
        norm_out[0],
        norm_out[1],
        norm_out[2],
    )


def solution(mesh):
    return jax.shard_map(
        body,
        mesh=mesh,
        in_specs=(
            P(("dp", "tensor"), None),
            P(("dp", "tensor"), None),
            P(),
            P(("dp", "tensor"), None),
            P(),
            P("dp", None, "tensor"),
            P("dp", None, "tensor"),
            P("dp", None, "tensor"),
            P("tensor", "dp"),
            P("tensor", "dp"),
            P("tensor", "dp"),
            P("dp", None, "tensor"),
            P("dp", None, "tensor"),
            P("dp", None, "tensor"),
            P(None, "tensor", "dp"),
            P(None, "tensor", "dp"),
            P(None, "tensor", "dp"),
            P(None, "tensor"),
            P(None, "tensor"),
            P(None, "tensor"),
            P(),
            P(),
            P(),
        ),
        out_specs=(
            P(("dp", "tensor"), None),
            P(("dp", "tensor"), None),
            P(),
            P("dp", None, "tensor"),
            P("dp", None, "tensor"),
            P("dp", None, "tensor"),
            P("tensor", "dp"),
            P("tensor", "dp"),
            P("tensor", "dp"),
            P("dp", None, "tensor"),
            P("dp", None, "tensor"),
            P("dp", None, "tensor"),
            P(None, "tensor", "dp"),
            P(None, "tensor", "dp"),
            P(None, "tensor", "dp"),
            P(None, "tensor"),
            P(None, "tensor"),
            P(None, "tensor"),
            P(),
            P(),
            P(),
        ),
        check_vma=False,
    )
```

time: 1270 us -> 673 us (0.53)
  waiting for transfers between devices: 674 us -> 210 us
  matrix products: 246 us -> 193 us
  local copies, waits for them, and re-layouts: 162 us -> 116 us
  blocking collectives: 66.5 us -> 46 us
  other arithmetic: 93.1 us -> 76.6 us
    all_gather x7 -> x2, waiting for transfers between devices: 241 us -> 40.4 us  [gather(): whole = lax.all_gather(block.astype(low_type), every, axis=0, tiled=True)]
    unnamed x15 -> x4, waiting for transfers between devices: 187 us -> 0.07 us
    reduce_scatter x6 -> x2, waiting for transfers between devices: 247 us -> 169 us  [scatter(): lax.psum_scatter(stacked, every, scatter_dimension=0, tiled=True)]
    reshape x11 -> x17, local copies, waits for them, and re-layouts: 79.6 us -> 50.8 us  [the longest x2 8.62 us: body(): (projected[:, :shard_width] + bias_t[0]).astype(low_type)]
    dot_general x4 -> x8, matrix products: 79.1 us -> 54.5 us  [the longest x2 20.5 us: body(): jnp.dot(cotangent, fc2_low[t], preferred_element_type=jnp.float32)]
    all_gather x1, blocking collectives: 26.5 us -> 5.6 us  [body(): split_whole_bias = lax.all_gather(split_bias, 'tensor', axis=0, tiled=False)]
    another operation x0 -> x10, other arithmetic: none -> 18.1 us  [the longest x6 17.1 us: scatter(): stacked = jnp.stack(parts).reshape(halves * model_width, parts[0].shape[1])]
    reduce_sum x3 -> x1, other arithmetic: 14.6 us -> 0.6 us  [body(): jnp.sum(norm_total * norm_total)]
  transfers between devices with their start and end apart: 14 -> 4, of which waited for: 13 -> 3; matrix products, arithmetic and copies ran while one was open for 25% -> 27% of each run, Pallas kernels for 0% -> 0%
where the time goes in v1:
time: 673 us; the launch traced here: 662 us
  waiting for transfers between devices  210 us (31%)
  matrix products  193 us (29%)
  local copies, waits for them, and re-layouts  116 us (17%)
  other arithmetic  76.6 us (11%)
  blocking collectives  46 us (7%)
  between operations  20.7 us (3%)
    reduce_scatter x2, waiting for transfers between devices, scatter(): lax.psum_scatter(stacked, every, scatter_dimension=0, tiled=True)  169 us
    dot_general x8, matrix products, dot_back(): lax.dot_general(left_side, right_side, (((1,), (1,)), ((), ())), preferre...  52.7 us
    dot_general x8, matrix products, transpose_dot(): lax.dot_general(left_side, right_side, (((0,), (0,)), ((), ())), preferre...  42.7 us
    psum x1, blocking collectives, body(): lax.psum((grad_norm_rows, grad_split, local_square), ('dp', 'tensor'))  40.4 us
    all_gather x2, waiting for transfers between devices, gather(): whole = lax.all_gather(block.astype(low_type), every, axis=0, tiled=True)  40.4 us
    unnamed x167, local copies, waits for them, and re-layouts  22.2 us
    dot_general x2, matrix products, body(): jnp.dot(cotangent, fc2_low[t], preferred_element_type=jnp.float32)  20.5 us
    sub x2, other arithmetic, body(): attention = jax.nn.softmax(scores, axis=-1)  17.9 us
  transfers between devices with their start and end apart: 4, of which 3 were waited for; matrix products, arithmetic and copies ran while one was open for 27% of the time, Pallas kernels for 0%

profile of v1, /device:TPU:0, one launch (start us, length us, event | category | flops | bytes accessed | tf_op | source)
XLA Modules:
  0.0 662.2 jit_solution(4477941152413452380)
XLA Ops:
  20.2 6.1 gather_fusion
  33.8 40.4 %all-gather.5.cloned.1.call-done = bf16[1536,1152]{1,0:T(8,128)(2,1)} async-done(((bf16[48,1152]{1,0:T(8,128)(2,1)}), bf16[1536,1152]{1,0:T(8,128)(2,1)}) %all-gather.5.cloned.1.call-update) | async-done | bytes 3538960 | tf_op jit(solution)/shard_map/all_gather | solution.py:101
  122.1 8.9 %fusion.109 = (f32[32,6,49]{2,1,0:T(8,128)S(1)}, f32[32,6,49,49]{2,3,1,0:T(8,128)S(1)}) fusion(f32[32,6,49,49]{2,3,1,0:T(8,128)S(1)} %fusion.53), kind=kOutput, calls=%fused_computation.231 | output fusion | flops 1844016 | bytes 3725568 | tf_op jit(solution)/shard_map/sub | solution.py:137
  146.2 8.9 %fusion.110 = (f32[32,6,49]{2,1,0:T(8,128)S(1)}, f32[32,6,49,49]{2,3,1,0:T(8,128)S(1)}) fusion(f32[32,6,49,49]{2,3,1,0:T(8,128)S(1)} %fusion.45), kind=kOutput, calls=%fused_computation.232 | output fusion | flops 1844016 | bytes 3725568 | tf_op jit(solution)/shard_map/sub | solution.py:137
  174.0 8.7 %multiply_convert_fusion = (bf16[1568,1536]{1,0:T(8,128)(2,1)}, f32[1568,1536]{1,0:T(8,128)}) fusion(f32[1536]{0:T(1024)S(1)} %add.329, bf16[1568,768]{1,0:T(8,128)(2,1)S(1)} %add_convert_fusion.1, bf16[2,768,3456]{2,1,0:T(8,128)(2,1)S(1)} %bitcast.204), kind=kOutput, calls=%fused_computation.21 | convolution fusion | flops 3713826816 | bytes 19226624 | tf_op jit(solution)/shard_map/dot_general | solution.py:156
  182.7 8.8 %multiply_convert_fusion.1 = (bf16[1568,1536]{1,0:T(8,128)(2,1)}, f32[1568,1536]{1,0:T(8,128)}) fusion(f32[1536]{0:T(1024)S(1)} %add.325, bf16[1568,768]{1,0:T(8,128)(2,1)S(1)} %add_convert_fusion.1, bf16[2,768,3456]{2,1,0:T(8,128)(2,1)S(1)} %bitcast.205), kind=kOutput, calls=%fused_computation.23 | convolution fusion | flops 3713826816 | bytes 19226624 | tf_op jit(solution)/shard_map/dot_general | solution.py:156
  191.6 11.1 %convert_reduce_fusion = (f32[1536]{0:T(1024)}, bf16[1568,1536]{1,0:T(8,128)(2,1)}) fusion(f32[1568,1536]{1,0:T(8,128)} %get-tuple-element.127, bf16[1568,768]{1,0:T(8,128)(2,1)S(1)} %copy-done.14, bf16[2,768,3456]{2,1,0:T(8,128)(2,1)S(1)} %bitcast.206), kind=kOutput, calls=%fused_computation.19 | convolution fusion | flops 3733092864 | bytes 19224576 | tf_op jit(solution)/shard_map/dot_general | solution.py:164
  202.6 9.4 %convert_reduce_fusion.1 = (f32[1536]{0:T(1024)}, bf16[1568,1536]{1,0:T(8,128)(2,1)S(1)}) fusion(f32[1568,1536]{1,0:T(8,128)} %get-tuple-element.125, bf16[1568,768]{1,0:T(8,128)(2,1)S(1)} %copy-done.14, bf16[2,768,3456]{2,1,0:T(8,128)(2,1)S(1)} %bitcast.207), kind=kOutput, calls=%fused_computation.20 | convolution fusion | flops 3733092864 | bytes 19224576 | tf_op jit(solution)/shard_map/dot_general | solution.py:164
  212.1 5.9 fusion.65
  218.0 9.9 %multiply_reduce_fusion.4 = (f32[768]{0:T(1024)S(1)}, f32[1568]{0:T(1024)S(1)}, f32[768]{0:T(1024)S(1)}, f32[1568,768]{1,0:T(8,128)S(1)}) fusion(f32[1568,768]{1,0:T(8,128)S(1)} %get-tuple-element.123, f32[1568]{0:T(1024)S(1)} %fusion.91, f32[1568]{0:T(1024)S(1)} %broadcast_multiply_fusion, f32[768]{0:T(1024)S(1)} %get-tuple-element.71, ...), kind=kOutput, calls=%fused_computation.50 | convolution fusion | flops 3710211072 | bytes 21654912 | tf_op jit(solution)/shard_map/dot_general | solution.py:45
  247.8 6.5 multiply_reduce_fusion
  269.3 6.5 multiply_reduce_fusion.1
  314.7 7.0 %convolution_convert_fusion.1 = bf16[768,1152]{1,0:T(8,128)(2,1)} fusion(bf16[1568,768]{1,0:T(8,128)(2,1)S(1)} %copy-done.27, bf16[1568,1152]{1,0:T(8,128)(2,1)} %constant_dynamic-update-slice_fusion), kind=kOutput, calls=%fused_computation.69 | convolution fusion | flops 2775416832 | bytes 7790592 | tf_op jit(solution)/shard_map/dot_general | solution.py:39
  338.1 5.9 convolution_convert_fusion
  348.1 7.7 %convolution_convert_fusion.3 = bf16[768,1536]{1,0:T(8,128)(2,1)S(1)} fusion(bf16[1568,768]{1,0:T(8,128)(2,1)} %copy-done.29, bf16[1568,1536]{1,0:T(8,128)(2,1)} %get-tuple-element.135), kind=kOutput, calls=%fused_computation.71 | convolution fusion | flops 3700555776 | bytes 9584640 | tf_op jit(solution)/shard_map/dot_general | solution.py:39
  355.9 7.3 %fusion.22 = bf16[768,1536]{1,0:T(8,128)(2,1)S(1)} fusion(bf16[1568,1536]{1,0:T(8,128)(2,1)} %get-tuple-element.126, bf16[1568,768]{1,0:T(8,128)(2,1)S(1)} %copy-done.15), kind=kOutput, calls=%fused_computation.76 | convolution fusion | flops 3700555776 | bytes 9584640 | tf_op jit(solution)/shard_map/dot_general | solution.py:39
  378.8 8.5 %pad_maximum_fusion = bf16[2,768,3072]{2,1,0:T(8,128)(2,1)} fusion(bf16[1,768,3072]{2,1,0:T(8,128)(2,1)} %maximum_bitcast_fusion.1, bf16[1,768,3072]{2,1,0:T(8,128)(2,1)} %maximum_bitcast_fusion), kind=kLoop, calls=%fused_computation.25 | loop fusion | flops 4718592 | bytes 18874368 | tf_op jit(solution)/shard_map/stack | solution.py:172
  388.5 8.3 %fusion.70 = f32[1568,768]{1,0:T(8,128)} fusion(bf16[1568,1152]{1,0:T(8,128)(2,1)} %constant_dynamic-update-slice_fusion, bf16[1536,1152]{1,0:T(8,128)(2,1)} %all-gather.5.cloned.1.call-done), kind=kOutput, calls=%fused_computation.136 | convolution fusion | flops 2774532096 | bytes 10199040 | tf_op jit(solution)/shard_map/dot_general | solution.py:45
  397.0 7.0 %multiply_reduce_fusion.5 = (f32[768]{0:T(1024)S(1)}, f32[1568]{0:T(1024)S(1)}, f32[768]{0:T(1024)S(1)}, f32[1568,768]{1,0:T(8,128)S(1)}) fusion(f32[1568,768]{1,0:T(8,128)S(1)} %bitcast.176, f32[1568]{0:T(1024)S(1)} %copy-done.50, f32[1568]{0:T(1024)S(1)} %copy-done.42, f32[768]{0:T(1024)S(1)} %copy-done.54, f32[1568,768]{1,0:T(8,128)} %fusion.70, ...), kind=kOutput, calls=%fused_computation.52 | convolution fusion | flops 2785367040 | bytes 19865728 | tf_op jit(solution)/shard_map/dot_general | solution.py:45
  408.9 7.0 %fusion.66 = f32[1568,768]{1,0:T(8,128)S(1)} fusion(bf16[1568,1536]{1,0:T(8,128)(2,1)} %get-tuple-element.124, bf16[2,768,3456]{2,1,0:T(8,128)(2,1)} %bitcast.200), kind=kOutput, calls=%fused_computation.132 | convolution fusion | flops 3699376128 | bytes 11993088 | tf_op jit(solution)/shard_map/dot_general | solution.py:45
  416.0 8.7 %add_convert_fusion = bf16[1568,768]{1,0:T(8,128)(2,1)} fusion(f32[1568,768]{1,0:T(8,128)S(1)} %bitcast.178, f32[1568,768]{1,0:T(8,128)S(1)} %fusion.66, bf16[1568,1536]{1,0:T(8,128)(2,1)} %get-tuple-element.126, f32[768]{0:T(1024)S(1)} %copy-done.57, bf16[2,768,3456]{2,1,0:T(8,128)(2,1)} %bitcast.201), kind=kOutput, calls=%fused_computation.56 | convolution fusion | flops 3704193024 | bytes 19221504 | tf_op jit(solution)/shard_map/dot_general | solution.py:45
  424.7 29.6 %reduce-scatter.3.cloned.1.call-done = bf16[48,1536]{1,0:T(8,128)(2,1)} async-done(((bf16[1536,1536]{1,0:T(8,128)(2,1)}), bf16[48,1536]{1,0:T(8,128)(2,1)}) %reduce-scatter.3.cloned.1.call-update) | async-done | bytes 147472 | tf_op jit(solution)/shard_map/reduce_scatter | solution.py:173
  455.9 139.5 %reduce-scatter.5.cloned.1.call-done = bf16[48,3072]{1,0:T(8,128)(2,1)} async-done(((bf16[1536,3072]{1,0:T(8,128)(2,1)}), bf16[48,3072]{1,0:T(8,128)(2,1)}) %reduce-scatter.5.cloned.1.call-update) | async-done | bytes 294928 | tf_op jit(solution)/shard_map/reduce_scatter | solution.py:173
  599.3 40.4 %all-reduce = (f32[]{:T(128)}, f32[6,768]{1,0:T(8,128)S(1)}, f32[2,6,384]{2,1,0:T(8,128)S(1)}) all-reduce(f32[]{:T(128)S(6)} %add.344, f32[6,768]{1,0:T(8,128)S(1)} %stack.60, f32[2,6,384]{2,1,0:T(8,128)S(1)} %pad_maximum_fusion.3), channel_id=1, replica_groups=mesh['dp'=16,'tensor'=2] {'dp','tensor'}, use_global_device_ids=true, to_apply=%region_18.19 | all-reduce | flops 9217 | bytes 73736 | tf_op jit(solution)/shard_map/psum | solution.py:253
  (308 shorter events, 233.2 us)
Async XLA Ops:
  7.2 13.0 %copy-start = (f32[196,768]{1,0:T(8,128)S(1)}, f32[196,768]{1,0:T(8,128)}, u32[]{:S(2)}) copy-start(f32[196,768]{1,0:T(8,128)} %param.25) | copy-start | bytes 1806340
  7.2 66.9 %all-gather.5.cloned.1.call-start = ((), (), s32[]{:S(2)}) async-start(), calls=%async_computation.2 | async-start | bytes 3649536 | tf_op jit(solution)/shard_map/all_gather | solution.py:101
  8.9 155.8 %all-gather.7.cloned.1.call-start = ((), (), s32[]{:S(2)}) async-start(), calls=%async_computation.3 | async-start | bytes 10948608 | tf_op jit(solution)/shard_map/all_gather | solution.py:101
  12.8 441.5 %reduce-scatter.3.cloned.1.call-start = ((), (), s32[]{:S(2)}) async-start(), calls=%async_computation.4 | async-start | bytes 4866048 | tf_op jit(solution)/shard_map/reduce_scatter | solution.py:173
  33.8 45.2 %copy-start.26 = (bf16[1568,768]{1,0:T(8,128)(2,1)}, bf16[1568,768]{1,0:T(8,128)(2,1)S(1)}, u32[]{:S(2)}) copy-start(bf16[1568,768]{1,0:T(8,128)(2,1)S(1)} %add_convert_fusion.2) | copy-start | bytes 7225348
  83.1 11.8 %slice-start.12 = ((s8[7225344]{0:T(1024)(128)(4,1)}), s8[3031040]{0:T(1024)(128)(4,1)S(1)}, s32[]{:S(2)}) async-start(s8[7225344]{0:T(1024)(128)(4,1)} %bitcast.187), calls=%async_computation.18 | async-start | bytes 6062080
  122.1 11.3 %copy-start.20 = (bf16[32,49,6,64]{3,2,1,0:T(8,128)(2,1)S(1)}, bf16[32,49,6,64]{3,2,1,0:T(8,128)(2,1)}, u32[]{:S(2)}) copy-start(bf16[32,49,6,64]{3,2,1,0:T(8,128)(2,1)} %reshape.273) | copy-start | bytes 3612676
  170.7 57.3 %copy-start.3 = (f32[1568,768]{1,0:T(8,128)}, f32[1568,768]{1,0:T(8,128)S(1)}, u32[]{:S(2)}) copy-start(f32[1568,768]{1,0:T(8,128)S(1)} %get-tuple-element.123) | copy-start | bytes 14450692
  242.8 11.5 %slice-start.10 = ((s8[5505024]{0:T(1024)(128)(4,1)}), s8[1310720]{0:T(1024)(128)(4,1)S(1)}, s32[]{:S(2)}) async-start(s8[5505024]{0:T(1024)(128)(4,1)} %bitcast.184), calls=%async_computation.16 | async-start | bytes 2621440
  262.7 13.1 %slice-start.8 = ((s8[5505024]{0:T(1024)(128)(4,1)}), s8[1310720]{0:T(1024)(128)(4,1)S(1)}, s32[]{:S(2)}) async-start(s8[5505024]{0:T(1024)(128)(4,1)} %bitcast.182), calls=%async_computation.14 | async-start | bytes 2621440
  347.9 247.5 %reduce-scatter.5.cloned.1.call-start = ((), (), s32[]{:S(2)}) async-start(), calls=%async_computation.5 | async-start | bytes 9732096 | tf_op jit(solution)/shard_map/reduce_scatter | solution.py:173
  348.1 18.1 %slice-start.17 = ((s8[4816896]{0:T(1024)(128)(4,1)}), s8[4194304]{0:T(1024)(128)(4,1)S(1)}, s32[]{:S(2)}) async-start(s8[4816896]{0:T(1024)(128)(4,1)} %bitcast.210), calls=%async_computation.23 | async-start | bytes 8388608
  355.9 10.3 %slice-start.18 = ((s8[4816896]{0:T(1024)(128)(4,1)}), s8[622592]{0:T(1024)(128)(4,1)S(1)}, s32[]{:S(2)}) async-start(s8[4816896]{0:T(1024)(128)(4,1)} %bitcast.210), calls=%async_computation.24 | async-start | bytes 1245184
  388.5 17.2 %slice-start.6 = ((s8[4816896]{0:T(1024)(128)(4,1)}), s8[4194304]{0:T(1024)(128)(4,1)S(1)}, s32[]{:S(2)}) async-start(s8[4816896]{0:T(1024)(128)(4,1)} %bitcast.179), calls=%async_computation.12 | async-start | bytes 8388608
  405.8 10.1 %slice-start.4 = ((s8[4816896]{0:T(1024)(128)(4,1)}), s8[622592]{0:T(1024)(128)(4,1)S(1)}, s32[]{:S(2)}) async-start(s8[4816896]{0:T(1024)(128)(4,1)} %bitcast.177), calls=%async_computation.10 | async-start | bytes 1245184
  416.0 228.3 %copy-start.44 = (f32[6,768]{1,0:T(8,128)S(1)}, f32[6,768]{1,0:T(8,128)}, u32[]{:S(2)}) copy-start(f32[6,768]{1,0:T(8,128)} %param.43) | copy-start | bytes 55300
  416.0 229.7 %copy-start.40 = (f32[384,48]{0,1:T(8,128)S(1)}, f32[384,48]{0,1:T(8,128)}, u32[]{:S(2)}) copy-start(f32[384,48]{0,1:T(8,128)} %param.31) | copy-start | bytes 221188
  424.6 222.7 %copy-start.52 = (f32[6,384]{1,0:T(8,128)S(1)}, f32[6,384]{1,0:T(8,128)}, u32[]{:S(2)}) copy-start(f32[6,384]{1,0:T(8,128)} %param.40) | copy-start | bytes 27652
  424.6 224.1 %copy-start.34 = (f32[48,3,384]{2,0,1:T(8,128)S(1)}, f32[48,3,384]{2,0,1:T(8,128)}, u32[]{:S(2)}) copy-start(f32[48,3,384]{2,0,1:T(8,128)} %param.28) | copy-start | bytes 663556
  424.6 226.0 %copy-start.32 = (f32[48,4,384]{2,1,0:T(4,128)S(1)}, f32[48,4,384]{2,1,0:T(4,128)}, u32[]{:S(2)}) copy-start(f32[48,4,384]{2,1,0:T(4,128)} %param.34) | copy-start | bytes 884740
  424.6 226.0 %copy-start.38 = (f32[48,4,384]{2,1,0:T(4,128)S(1)}, f32[48,4,384]{2,1,0:T(4,128)}, u32[]{:S(2)}) copy-start(f32[48,4,384]{2,1,0:T(4,128)} %param.36) | copy-start | bytes 884740
  424.6 226.0 %copy-start.39 = (f32[48,4,384]{2,1,0:T(4,128)S(1)}, f32[48,4,384]{2,1,0:T(4,128)}, u32[]{:S(2)}) copy-start(f32[48,4,384]{2,1,0:T(4,128)} %param.35) | copy-start | bytes 884740
  424.7 227.3 %copy-start.33 = (f32[4,384,48]{1,2,0:T(8,128)S(1)}, f32[4,384,48]{1,2,0:T(8,128)}, u32[]{:S(2)}) copy-start(f32[4,384,48]{1,2,0:T(8,128)} %param.37) | copy-start | bytes 884740
  643.0 11.1 %copy-start.1 = (f32[196,768]{1,0:T(8,128)S(1)}, f32[196,768]{1,0:T(8,128)}, u32[]{:S(2)}) copy-start(f32[196,768]{1,0:T(8,128)} %param.25) | copy-start | bytes 1806340
  (61 other events, 324.2 us)
Sparse Core Ops, SparseCore 0:
  11.5 62.6 all-gather.4
  77.1 85.4 all-gather.6
  348.0 106.1 reduce-scatter.2
  460.0 135.3 reduce-scatter.4
